TPU v7x, 256 devices: a whole 4x4x8 slice. The times are simulated.
256 devices in a mesh: dp: 4 (over z_hi, core), expert: 64 (over x, y, z_lo).
Axes of the slice: x: 4, y: 4, z: 8 (z_hi: 2, z_lo: 4; z = z_hi * 4 + z_lo), core: 2. Of those that a mesh axis runs over, the one named last changes fastest.
Arguments:
- query: bfloat16 [2, 16384, 2560], P(None, ('dp', 'expert')), may hold values from -24 to 24
- keys: bfloat16 [2, 16384, 512], P(None, ('dp', 'expert')), may hold values from -4 to 4
- values: bfloat16 [2, 16384, 512], P(None, ('dp', 'expert')), may hold values from -6 to 6
- lengths: int32 [2, 256, 4], P(None, ('dp', 'expert')), may hold values from 0 to 64, as said below
- routes: int32 [2, 16384, 6], P(None, ('dp', 'expert')), may hold values from 0 to 63, as said below
- gates: float32 [2, 16384, 6], P(None, ('dp', 'expert')), may hold values from 0.05 to 0.4
- norm_gain: float32 [2560], replicated, may hold values from 0.1 to 1.9
- old_holds: int32 [64], replicated, may hold values from 0 to 63, as said below
- dup_experts: int32 [4], replicated, may hold values from 0 to 63, as said below
- w_gate: bfloat16 [64, 2560, 768], P('expert'), may hold values from -0.125 to 0.125
- w_up: bfloat16 [64, 2560, 768], P('expert'), may hold values from -0.125 to 0.125
- w_down: bfloat16 [64, 768, 2560], P('expert'), may hold values from -0.21875 to 0.21875
Outputs:
- layer_out: bfloat16 [2, 16384, 2560], P(None, ('dp', 'expert'))
Inputs may be any that keep to these rules, and one draw needn't show every extreme that they name: Each length is a multiple of 8; the 4 lengths of one device in one batch add up to 64. `routes`: each token names 6 different experts. `dup_experts`: 4 different experts. `old_holds`: each expert stands in exactly one slot.
All inputs are finite; a program needn't handle non-finite values.
Results may differ from a plain program's by a relative error of at most 0.0061.
Values may be sent and summed in bfloat16 or wider, within the bound.
A program may use at most 128 MiB of HBM per device.

v0:
```python
import jax
import jax.numpy as jnp
from jax import lax
from jax.sharding import PartitionSpec as P

HEAD_WIDTH = 128
CAP = 6


def from_behind(value, axis, steps):
    count = lax.axis_size(axis)
    pairs = [(source, (source + steps) % count) for source in range(count)]
    return lax.ppermute(value, axis, pairs)


def attend(query, key_rows, value_rows, lengths):
    rows = query.shape[0]
    kv_heads = key_rows.shape[1] // HEAD_WIDTH
    query_group = query.shape[1] // HEAD_WIDTH // kv_heads
    ends = jnp.cumsum(lengths)
    position = lax.iota(jnp.int32, rows)
    request = jnp.sum((position[:, None] >= ends[None, :]).astype(jnp.int32), axis=1)
    allowed = (request[:, None] == request[None, :]) & (position[None, :] <= position[:, None])
    query_heads = query.reshape(rows, kv_heads, query_group, HEAD_WIDTH)
    key_heads = key_rows.reshape(rows, kv_heads, HEAD_WIDTH)
    value_heads = value_rows.reshape(rows, kv_heads, HEAD_WIDTH)
    router_logits = jnp.einsum(
        "qhgd,khd->hgqk", query_heads, key_heads, preferred_element_type=jnp.float32
    ) * HEAD_WIDTH ** (-0.5)
    router_logits = jnp.where(allowed[None, None], router_logits, -1e30)
    highest = jnp.max(router_logits, axis=-1, keepdims=True)
    weights = jnp.exp(router_logits - highest)
    probs = (weights / jnp.sum(weights, axis=-1, keepdims=True)).astype(jnp.bfloat16)
    mixed = jnp.einsum("hgqk,khd->qhgd", probs, value_heads, preferred_element_type=jnp.float32)
    return mixed.reshape(rows, kv_heads * query_group * HEAD_WIDTH)


def normalize(attn, gain):
    meansq = jnp.mean(attn * attn, axis=-1, keepdims=True)
    return (attn * lax.rsqrt(meansq + 1e-05) * gain).astype(jnp.bfloat16)


def expert_rows(rows, gate_mat, up_mat, down_mat):
    gate_val = jnp.dot(rows, gate_mat, preferred_element_type=jnp.float32)
    up_val = jnp.dot(rows, up_mat, preferred_element_type=jnp.float32)
    hidden = (jax.nn.silu(gate_val) * up_val).astype(jnp.bfloat16)
    return jnp.dot(hidden, down_mat, preferred_element_type=jnp.float32).astype(jnp.bfloat16)


def routing(routes, copies_of, first_target, second_target, regions):
    expert_list = lax.iota(jnp.int32, copies_of.shape[0])
    hit = (routes[:, :, None] == expert_list[None, None, :]).astype(jnp.int32)
    named = jnp.sum(hit, axis=1)
    before = jnp.cumsum(named, axis=0) - named
    place = jnp.sum(hit * before[:, None, :], axis=2)
    limit = jnp.sum(hit * copies_of[None, None, :], axis=2)
    kept = place < limit * CAP
    which = place // CAP
    target = jnp.where(
        which == 0,
        jnp.sum(hit * first_target[None, None, :], axis=2),
        jnp.sum(hit * second_target[None, None, :], axis=2),
    )
    flat = (target * regions + which) * CAP + place % CAP
    return (flat, kept)


def pack(normed, flat, kept, slots):
    tok_rows = normed.shape[0]
    token = jnp.broadcast_to(lax.iota(jnp.int32, tok_rows)[:, None], flat.shape)
    spot = jnp.where(kept, flat, slots)
    source_row = jnp.full((slots,), tok_rows, jnp.int32).at[spot].set(token, mode="drop")
    padded = jnp.concatenate([normed, jnp.zeros((1, normed.shape[1]), normed.dtype)], axis=0)
    return (padded[source_row], spot)


def combine(attn, returned, spot, kept, gates):
    picked = returned[jnp.minimum(spot, returned.shape[0] - 1)]
    weight = jnp.where(kept, gates, 0.0)
    mixed = jnp.einsum("tk,tkd->td", weight, picked.astype(jnp.float32))
    return (attn + mixed).astype(jnp.bfloat16)


def shards(
    query,
    keys,
    values,
    lengths,
    routes,
    gates,
    norm_gain,
    old_holds,
    dup_experts,
    w_gate,
    w_up,
    w_down,
):
    width = lax.axis_size("expert")
    half = width // 2
    features = norm_gain.shape[0]
    expert_list = lax.iota(jnp.int32, old_holds.shape[0])
    holder = jnp.sum(
        expert_list[:, None] * (old_holds[:, None] == expert_list[None, :]).astype(jnp.int32),
        axis=0,
    )
    doubled = jnp.sum((dup_experts[:, None] == expert_list[None, :]).astype(jnp.int32), axis=0)
    own_gate, own_up, own_down = (w_gate[0], w_up[0], w_down[0])
    moved = from_behind((w_gate, w_up, w_down), "expert", half)
    extra_gate, extra_up, extra_down = (moved[0][0], moved[1][0], moved[2][0])
    spare = (holder + half) % width
    position_now = lax.axis_index("expert")
    serving = jnp.sum(doubled * (spare == position_now).astype(jnp.int32)) > 0
    attn_one = attend(query[0], keys[0], values[0], lengths[0, 0])
    normed_one = normalize(attn_one, norm_gain)
    flat_one, kept_one = routing(routes[0], jnp.ones_like(doubled), holder, holder, 1)
    packed_one, spot_one = pack(normed_one, flat_one, kept_one, width * CAP)
    received = lax.all_to_all(
        packed_one.reshape(width, 1, CAP, features),
        "expert",
        split_axis=0,
        concat_axis=0,
        tiled=True,
    )
    result = expert_rows(received.reshape(-1, features), own_gate, own_up, own_down)
    back_one = lax.all_to_all(
        result.reshape(received.shape), "expert", split_axis=0, concat_axis=0, tiled=True
    )
    out_one = combine(attn_one, back_one.reshape(-1, features), spot_one, kept_one, gates[0])
    attn_two = attend(query[1], keys[1], values[1], lengths[1, 0])
    normed_two = normalize(attn_two, norm_gain)
    flat_two, kept_two = routing(routes[1], 1 + doubled, holder, spare, 2)
    packed_two, spot_two = pack(normed_two, flat_two, kept_two, width * 2 * CAP)
    received = lax.all_to_all(
        packed_two.reshape(width, 2, CAP, features),
        "expert",
        split_axis=0,
        concat_axis=0,
        tiled=True,
    )
    first_rows = received[:, 0]
    second_rows = received[:, 1]
    first_out = expert_rows(first_rows.reshape(-1, features), own_gate, own_up, own_down)
    second_flat = second_rows.reshape(-1, features)
    second_out = lax.cond(
        serving,
        lambda rows_in: expert_rows(rows_in, extra_gate, extra_up, extra_down),
        lambda rows_in: jnp.zeros_like(rows_in),
        second_flat,
    )
    result = jnp.stack(
        [first_out.reshape(first_rows.shape), second_out.reshape(second_rows.shape)], axis=1
    )
    back_two = lax.all_to_all(result, "expert", split_axis=0, concat_axis=0, tiled=True)
    out_two = combine(attn_two, back_two.reshape(-1, features), spot_two, kept_two, gates[1])
    return jnp.stack([out_one, out_two])


def solution(mesh):
    placed = (
        P(None, ("dp", "expert"), None),
        P(None, ("dp", "expert"), None),
        P(None, ("dp", "expert"), None),
        P(None, ("dp", "expert"), None),
        P(None, ("dp", "expert"), None),
        P(None, ("dp", "expert"), None),
        P(),
        P(),
        P(),
        P("expert", None, None),
        P("expert", None, None),
        P("expert", None, None),
    )
    return jax.shard_map(
        shards,
        mesh=mesh,
        in_specs=placed,
        out_specs=P(None, ("dp", "expert"), None),
        check_vma=False,
    )
```

profile of v0, /device:TPU:8, one launch (start us, length us, event | category | flops | bytes accessed | tf_op | source)
XLA Modules:
  0.0 577.7 jit_solution(1016598174687846322)
XLA Ops:
  19.1 12.0 %all-to-all-start = ((bf16[64,1,6,2560]{3,2,1,0:T(8,128)(2,1)}), bf16[64,1,6,2560]{3,2,1,0:T(8,128)(2,1)S(1)}, u32[]{:S(2)}, u32[]{:S(2)}) async-start(bf16[64,1,6,2560]{3,2,1,0:T(8,128)(2,1)} %bitcast.216), calls=%async_computation | async-start | bytes 5242880 | tf_op jit(solution)/shard_map/all_to_all | solution.py:117
  34.6 4.6 gather_fusion.2
  39.2 7.2 %reshape.457 = bf16[64,2,6,2560]{3,2,1,0:T(8,128)(2,1)} reshape(bf16[768,2560]{1,0:T(8,128)(2,1)} %gather_fusion.2) | data formatting | bytes 7864320 | tf_op jit(solution)/shard_map/reshape | solution.py:134
  46.3 7.4 %copy.86 = bf16[64,2,6,2560]{3,1,2,0:T(2,128)(2,1)} copy(bf16[64,2,6,2560]{3,2,1,0:T(8,128)(2,1)} %reshape.457) | data formatting | bytes 7864320 | tf_op jit(solution)/shard_map/reshape | solution.py:134
  53.8 39.4 %all-to-all-done = bf16[64,1,6,2560]{3,2,1,0:T(8,128)(2,1)S(1)} async-done(((bf16[64,1,6,2560]{3,2,1,0:T(8,128)(2,1)}), bf16[64,1,6,2560]{3,2,1,0:T(8,128)(2,1)S(1)}, u32[]{:S(2)}, u32[]{:S(2)}) %all-to-all-start) | async-done | bytes 1966112 | tf_op jit(solution)/shard_map/all_to_all | solution.py:117
  93.2 6.4 %all-to-all-start.2 = ((bf16[64,2,6,2560]{3,1,2,0:T(2,128)(2,1)}), bf16[64,2,6,2560]{3,1,2,0:T(2,128)(2,1)}, u32[]{:S(2)}, u32[]{:S(2)}) async-start(bf16[64,2,6,2560]{3,1,2,0:T(2,128)(2,1)} %copy.86), calls=%async_computation.2 | async-start | bytes 7864320 | tf_op jit(solution)/shard_map/all_to_all | solution.py:133
  108.5 5.5 fusion.25
  114.1 9.2 %convolution_convert_fusion.2 = bf16[384,2560]{1,0:T(8,128)(2,1)} fusion(bf16[1,768,2560]{2,1,0:T(8,128)(2,1)} %param.25, bf16[384,2560]{1,0:T(8,128)(2,1)S(1)} %copy-done.5, bf16[1,2560,768]{2,1,0:T(8,128)(2,1)} %param.24, f32[384,768]{1,0:T(8,128)} %fusion.25), kind=kOutput, calls=%fused_computation.20 | convolution fusion | flops 3022651392 | bytes 12976128 | tf_op jit(solution)/shard_map/dot_general | solution.py:47
  123.2 4.1 reshape.452
  127.3 61.4 %all-to-all-done.2 = bf16[64,2,6,2560]{3,1,2,0:T(2,128)(2,1)} async-done(((bf16[64,2,6,2560]{3,1,2,0:T(2,128)(2,1)}), bf16[64,2,6,2560]{3,1,2,0:T(2,128)(2,1)}, u32[]{:S(2)}, u32[]{:S(2)}) %all-to-all-start.2) | async-done | bytes 3932192 | tf_op jit(solution)/shard_map/all_to_all | solution.py:133
  188.7 6.6 %all-to-all-start.1 = ((bf16[64,1,6,2560]{3,2,1,0:T(8,128)(2,1)}), bf16[64,1,6,2560]{3,2,1,0:T(8,128)(2,1)}, u32[]{:S(2)}, u32[]{:S(2)}) async-start(bf16[64,1,6,2560]{3,2,1,0:T(8,128)(2,1)} %bitcast.21), calls=%async_computation.1 | async-start | bytes 5242880 | tf_op jit(solution)/shard_map/all_to_all | solution.py:125
  196.0 12.6 %slice_reduce_fusion = bf16[64,6,2560]{2,1,0:T(8,128)(2,1)S(1)} fusion(bf16[64,2,6,2560]{3,1,2,0:T(2,128)(2,1)} %all-to-all-done.2), kind=kLoop, calls=%fused_computation.21 | loop fusion | bytes 3932160 | tf_op jit(solution)/shard_map/slice | solution.py:140
  210.7 5.6 fusion.23
  216.3 9.2 %convolution_convert_fusion.1 = bf16[384,2560]{1,0:T(8,128)(2,1)} fusion(bf16[1,768,2560]{2,1,0:T(8,128)(2,1)} %param.25, bf16[384,2560]{1,0:T(8,128)(2,1)S(1)} %copy-done.6, bf16[1,2560,768]{2,1,0:T(8,128)(2,1)} %param.24, f32[384,768]{1,0:T(8,128)} %fusion.23), kind=kOutput, calls=%fused_computation.19 | convolution fusion | flops 3022651392 | bytes 12976128 | tf_op jit(solution)/shard_map/dot_general | solution.py:47
  225.5 4.1 stack_reshape.10
  229.6 22.8 %collective-permute-done = bf16[1,2560,768]{2,1,0:T(8,128)(2,1)} collective-permute-done((bf16[1,2560,768]{2,1,0:T(8,128)(2,1)}, bf16[1,2560,768]{2,1,0:T(8,128)(2,1)}, u32[]{:S(2)}, u32[]{:S(2)}) %collective-permute-start) | collective-permute-done | bytes 3932192 | tf_op jit(solution)/shard_map/ppermute | solution.py:13
  252.4 84.7 %collective-permute-done.1 = bf16[1,2560,768]{2,1,0:T(8,128)(2,1)} collective-permute-done((bf16[1,2560,768]{2,1,0:T(8,128)(2,1)}, bf16[1,2560,768]{2,1,0:T(8,128)(2,1)}, u32[]{:S(2)}, u32[]{:S(2)}) %collective-permute-start.1) | collective-permute-done | bytes 3932192 | tf_op jit(solution)/shard_map/ppermute | solution.py:13
  337.1 84.2 %collective-permute-done.2 = bf16[1,768,2560]{2,1,0:T(8,128)(2,1)} collective-permute-done((bf16[1,768,2560]{2,1,0:T(8,128)(2,1)}, bf16[1,768,2560]{2,1,0:T(8,128)(2,1)}, u32[]{:S(2)}, u32[]{:S(2)}) %collective-permute-start.2) | collective-permute-done | bytes 3932192 | tf_op jit(solution)/shard_map/ppermute | solution.py:13
  427.3 6.0 %copy.88 = bf16[64,2,6,2560]{3,1,2,0:T(2,128)(2,1)} copy(bf16[64,2,6,2560]{3,2,0,1:T(8,128)(2,1)S(1)} %pad_maximum_fusion) | data formatting | bytes 7864320 | tf_op jit(solution)/shard_map/stack | solution.py:150
  433.3 29.8 %all-to-all-start.3 = ((bf16[64,2,6,2560]{3,1,2,0:T(2,128)(2,1)}), bf16[64,2,6,2560]{3,1,2,0:T(2,128)(2,1)}, u32[]{:S(2)}, u32[]{:S(2)}) async-start(bf16[64,2,6,2560]{3,1,2,0:T(2,128)(2,1)} %copy.88), calls=%async_computation.3 | async-start | bytes 7864320 | tf_op jit(solution)/shard_map/all_to_all | solution.py:153
  473.8 77.1 %all-to-all-done.3 = bf16[64,2,6,2560]{3,1,2,0:T(2,128)(2,1)} async-done(((bf16[64,2,6,2560]{3,1,2,0:T(2,128)(2,1)}), bf16[64,2,6,2560]{3,1,2,0:T(2,128)(2,1)}, u32[]{:S(2)}, u32[]{:S(2)}) %all-to-all-start.3) | async-done | bytes 3932192 | tf_op jit(solution)/shard_map/all_to_all | solution.py:153
  550.9 5.7 copy.89
  556.6 7.2 %reshape.458 = bf16[768,2560]{1,0:T(8,128)(2,1)} reshape(bf16[64,2,6,2560]{3,2,1,0:T(8,128)(2,1)} %copy.89) | data formatting | bytes 7864320 | tf_op jit(solution)/shard_map/reshape | solution.py:154
  563.8 7.8 %gather_fusion.3 = bf16[384,2560]{1,0:T(8,128)(2,1)S(1)} fusion(bf16[768,2560]{1,0:T(8,128)(2,1)} %reshape.458, s32[1024]{0:T(1024)S(1)} %pad_clamp_fusion), kind=kCustom, calls=%fused_computation.3 | custom fusion | bytes 3933696 | tf_op jit(solution)/shard_map/gather | solution.py:78
  (115 shorter events, 55.8 us)
Async XLA Ops:
  3.9 2.1 copy-start.8
  6.1 1.1 copy-start.12
  6.1 1.2 copy-start.10
  6.5 1.2 copy-start.13
  7.2 6.8 %copy-start.1 = (f32[64,2560]{1,0:T(8,128)}, f32[64,2560]{1,0:T(8,128)S(1)}, u32[]{:S(2)}) copy-start(f32[64,2560]{1,0:T(8,128)S(1)} %reshape.456) | copy-start | bytes 1966084
  8.3 5.7 copy-start.9
  8.9 5.3 copy-start.3
  19.1 74.0 %all-to-all-start = ((bf16[64,1,6,2560]{3,2,1,0:T(8,128)(2,1)}), bf16[64,1,6,2560]{3,2,1,0:T(8,128)(2,1)S(1)}, u32[]{:S(2)}, u32[]{:S(2)}) async-start(bf16[64,1,6,2560]{3,2,1,0:T(8,128)(2,1)} %bitcast.216), calls=%async_computation | async-start | bytes 5242880 | tf_op jit(solution)/shard_map/all_to_all | solution.py:117
  93.2 95.6 %all-to-all-start.2 = ((bf16[64,2,6,2560]{3,1,2,0:T(2,128)(2,1)}), bf16[64,2,6,2560]{3,1,2,0:T(2,128)(2,1)}, u32[]{:S(2)}, u32[]{:S(2)}) async-start(bf16[64,2,6,2560]{3,1,2,0:T(2,128)(2,1)} %copy.86), calls=%async_computation.2 | async-start | bytes 7864320 | tf_op jit(solution)/shard_map/all_to_all | solution.py:133
  99.6 152.8 %collective-permute-start = (bf16[1,2560,768]{2,1,0:T(8,128)(2,1)}, bf16[1,2560,768]{2,1,0:T(8,128)(2,1)}, u32[]{:S(2)}, u32[]{:S(2)}) collective-permute-start(bf16[1,2560,768]{2,1,0:T(8,128)(2,1)} %param.23), channel_id=1, source_target_pairs={{0,32},{1,33},{2,34},{3,35},{4,36},{5,37},{6,38},{7,39},{8,40},{9,... | collective-permute-start | bytes 11796488 | tf_op jit(solution)/shard_map/ppermute | solution.py:13
  102.9 234.2 %collective-permute-start.1 = (bf16[1,2560,768]{2,1,0:T(8,128)(2,1)}, bf16[1,2560,768]{2,1,0:T(8,128)(2,1)}, u32[]{:S(2)}, u32[]{:S(2)}) collective-permute-start(bf16[1,2560,768]{2,1,0:T(8,128)(2,1)} %param.24), channel_id=1, source_target_pairs={{0,32},{1,33},{2,34},{3,35},{4,36},{5,37},{6,38},{7,39},{8,40},{9,... | collective-permute-start | bytes 11796488 | tf_op jit(solution)/shard_map/ppermute | solution.py:13
  103.2 318.1 %collective-permute-start.2 = (bf16[1,768,2560]{2,1,0:T(8,128)(2,1)}, bf16[1,768,2560]{2,1,0:T(8,128)(2,1)}, u32[]{:S(2)}, u32[]{:S(2)}) collective-permute-start(bf16[1,768,2560]{2,1,0:T(8,128)(2,1)} %param.25), channel_id=1, source_target_pairs={{0,32},{1,33},{2,34},{3,35},{4,36},{5,37},{6,38},{7,39},{8,40},{9,... | collective-permute-start | bytes 11796488 | tf_op jit(solution)/shard_map/ppermute | solution.py:13
  108.5 5.6 copy-start.5
  188.7 244.6 %all-to-all-start.1 = ((bf16[64,1,6,2560]{3,2,1,0:T(8,128)(2,1)}), bf16[64,1,6,2560]{3,2,1,0:T(8,128)(2,1)}, u32[]{:S(2)}, u32[]{:S(2)}) async-start(bf16[64,1,6,2560]{3,2,1,0:T(8,128)(2,1)} %bitcast.21), calls=%async_computation.1 | async-start | bytes 5242880 | tf_op jit(solution)/shard_map/all_to_all | solution.py:125
  210.7 5.6 copy-start.6
  421.9 1.5 copy-start
  433.3 29.9 %copy-start.11 = (f32[2,64,6]{1,0,2:T(2,128)S(1)}, f32[2,64,6]{1,0,2:T(2,128)}, u32[]{:S(2)}) copy-start(f32[2,64,6]{1,0,2:T(2,128)} %param.19) | copy-start | bytes 9220
  433.3 117.6 %all-to-all-start.3 = ((bf16[64,2,6,2560]{3,1,2,0:T(2,128)(2,1)}), bf16[64,2,6,2560]{3,1,2,0:T(2,128)(2,1)}, u32[]{:S(2)}, u32[]{:S(2)}) async-start(bf16[64,2,6,2560]{3,1,2,0:T(2,128)(2,1)} %copy.88), calls=%async_computation.3 | async-start | bytes 7864320 | tf_op jit(solution)/shard_map/all_to_all | solution.py:153
  472.6 1.1 copy-start.4
  573.9 2.6 copy-start.2
where the time goes:
time: 587 us; the launch traced here: 578 us
  waiting for transfers between devices  370 us (63%)
  local copies, waits for them, and re-layouts  101 us (17%)
  starting transfers between devices  61.7 us (11%)
  matrix products  35.7 us (6%)
  other arithmetic  8.2 us (1%)
    ppermute x3, waiting for transfers between devices, from_behind(): return lax.ppermute(value, axis, pairs)  192 us
    all_to_all x1, waiting for transfers between devices, shards(): lax.all_to_all(result, 'expert', split_axis=0, concat_axis=0, tiled=True)  77.1 us
    all_to_all x1, waiting for transfers between devices, shards(): lax.all_to_all(packed_two.reshape(width, 2, CAP, features), 'expert', spl...  61.4 us
    all_to_all x1, waiting for transfers between devices, shards(): lax.all_to_all(packed_one.reshape(width, 1, CAP, features), 'expert', spl...  39.4 us
    all_to_all x1, starting transfers between devices, shards(): lax.all_to_all(result, 'expert', split_axis=0, concat_axis=0, tiled=True)  29.8 us
    dot_general x2, matrix products, expert_rows(): jnp.dot(hidden, down_mat, preferred_element_type=jnp.float32)  18.4 us
    gather x4, local copies, waits for them, and re-layouts, combine(): picked = returned[jnp.minimum(spot, returned.shape[0] - 1)]  16 us
    reshape x2, local copies, waits for them, and re-layouts, shards(): packed_two.reshape(width, 2, CAP, features)  14.6 us
  transfers between devices with their start and end apart: 7, of which 6 were waited for; matrix products, arithmetic and copies ran while one was open for 17% of the time, Pallas kernels for 0%

commit v1 on v0

v1 whole, which is shorter than its diff:
```python
import jax
import jax.numpy as jnp
from jax import lax
from jax.sharding import PartitionSpec as P

HEAD_WIDTH = 128
CAP = 6


def attend(query, key_rows, value_rows, lengths):
    rows = query.shape[0]
    kv_heads = key_rows.shape[1] // HEAD_WIDTH
    query_group = query.shape[1] // HEAD_WIDTH // kv_heads
    ends = jnp.cumsum(lengths)
    position = lax.iota(jnp.int32, rows)
    request = jnp.sum((position[:, None] >= ends[None, :]).astype(jnp.int32), axis=1)
    allowed = (request[:, None] == request[None, :]) & (position[None, :] <= position[:, None])
    query_heads = query.reshape(rows, kv_heads, query_group, HEAD_WIDTH)
    key_heads = key_rows.reshape(rows, kv_heads, HEAD_WIDTH)
    value_heads = value_rows.reshape(rows, kv_heads, HEAD_WIDTH)
    router_logits = jnp.einsum(
        "qhgd,khd->hgqk", query_heads, key_heads, preferred_element_type=jnp.float32
    ) * HEAD_WIDTH ** (-0.5)
    router_logits = jnp.where(allowed[None, None], router_logits, -1e30)
    highest = jnp.max(router_logits, axis=-1, keepdims=True)
    weights = jnp.exp(router_logits - highest)
    probs = (weights / jnp.sum(weights, axis=-1, keepdims=True)).astype(jnp.bfloat16)
    mixed = jnp.einsum("hgqk,khd->qhgd", probs, value_heads, preferred_element_type=jnp.float32)
    return mixed.reshape(rows, kv_heads * query_group * HEAD_WIDTH)


def normalize(attn, gain):
    meansq = jnp.mean(attn * attn, axis=-1, keepdims=True)
    return (attn * lax.rsqrt(meansq + 1e-05) * gain).astype(jnp.bfloat16)


def expert_rows(rows, gate_mat, up_mat, down_mat):
    gate_val = jnp.dot(rows, gate_mat, preferred_element_type=jnp.float32)
    up_val = jnp.dot(rows, up_mat, preferred_element_type=jnp.float32)
    hidden = (jax.nn.silu(gate_val) * up_val).astype(jnp.bfloat16)
    return jnp.dot(hidden, down_mat, preferred_element_type=jnp.float32).astype(jnp.bfloat16)


def routing(routes, copies_of, holder):
    expert_list = lax.iota(jnp.int32, copies_of.shape[0])
    hit = (routes[:, :, None] == expert_list[None, None, :]).astype(jnp.int32)
    named = jnp.sum(hit, axis=1)
    before = jnp.cumsum(named, axis=0) - named
    place = jnp.sum(hit * before[:, None, :], axis=2)
    limit = jnp.sum(hit * copies_of[None, None, :], axis=2)
    kept = place < limit * CAP
    target = jnp.sum(hit * holder[None, None, :], axis=2)
    return (target, place, kept)


def combine(attn, returned, spot, kept, gates):
    picked = returned[jnp.minimum(spot, returned.shape[0] - 1)]
    weight = jnp.where(kept, gates, 0.0)
    mixed = jnp.einsum("tk,tkd->td", weight, picked.astype(jnp.float32))
    return (attn + mixed).astype(jnp.bfloat16)


def shards(
    query,
    keys,
    values,
    lengths,
    routes,
    gates,
    norm_gain,
    old_holds,
    dup_experts,
    w_gate,
    w_up,
    w_down,
):
    width = lax.axis_size("expert")
    features = norm_gain.shape[0]
    tokens = query.shape[1]
    per_dest = 3 * CAP
    slots = width * per_dest
    expert_list = lax.iota(jnp.int32, old_holds.shape[0])
    holder = jnp.sum(
        expert_list[:, None] * (old_holds[:, None] == expert_list[None, :]).astype(jnp.int32),
        axis=0,
    )
    doubled = jnp.sum((dup_experts[:, None] == expert_list[None, :]).astype(jnp.int32), axis=0)
    attn_one = attend(query[0], keys[0], values[0], lengths[0, 0])
    attn_two = attend(query[1], keys[1], values[1], lengths[1, 0])
    normed = normalize(jnp.concatenate([attn_one, attn_two], axis=0), norm_gain)
    target_one, place_one, kept_one = routing(routes[0], jnp.ones_like(doubled), holder)
    target_two, place_two, kept_two = routing(routes[1], 1 + doubled, holder)
    spot_one = jnp.where(kept_one, target_one * per_dest + place_one, slots)
    spot_two = jnp.where(kept_two, target_two * per_dest + CAP + place_two, slots)
    token = lax.iota(jnp.int32, tokens)[:, None]
    token_one = jnp.broadcast_to(token, spot_one.shape)
    token_two = jnp.broadcast_to(token + tokens, spot_two.shape)
    source_row = (
        jnp.full((slots,), 2 * tokens, jnp.int32)
        .at[spot_one].set(token_one, mode="drop")
        .at[spot_two].set(token_two, mode="drop")
    )
    padded = jnp.concatenate([normed, jnp.zeros((1, features), normed.dtype)], axis=0)
    packed = padded[source_row]
    received = lax.all_to_all(
        packed.reshape(width, per_dest, features),
        "expert",
        split_axis=0,
        concat_axis=0,
        tiled=True,
    )
    result = expert_rows(received.reshape(-1, features), w_gate[0], w_up[0], w_down[0])
    back = lax.all_to_all(
        result.reshape(received.shape), "expert", split_axis=0, concat_axis=0, tiled=True
    ).reshape(-1, features)
    out_one = combine(attn_one, back, spot_one, kept_one, gates[0])
    out_two = combine(attn_two, back, spot_two, kept_two, gates[1])
    return jnp.stack([out_one, out_two])


def solution(mesh):
    placed = (
        P(None, ("dp", "expert"), None),
        P(None, ("dp", "expert"), None),
        P(None, ("dp", "expert"), None),
        P(None, ("dp", "expert"), None),
        P(None, ("dp", "expert"), None),
        P(None, ("dp", "expert"), None),
        P(),
        P(),
        P(),
        P("expert", None, None),
        P("expert", None, None),
        P("expert", None, None),
    )
    return jax.shard_map(
        shards,
        mesh=mesh,
        in_specs=placed,
        out_specs=P(None, ("dp", "expert"), None),
        check_vma=False,
    )
```

time: 587 us -> 488 us (0.83)
  waiting for transfers between devices: 370 us -> 172 us
  blocking collectives: 0 us -> 187 us
  starting transfers between devices: 61.7 us -> 6.68 us
  local copies, waits for them, and re-layouts: 101 us -> 76.9 us
    ppermute x3 -> x0, waiting for transfers between devices: 192 us -> none  [from_behind(): return lax.ppermute(value, axis, pairs)]
    all_to_all x0 -> x1, blocking collectives: none -> 187 us  [shards(): lax.all_to_all(packed.reshape(width, per_dest, features), 'expert', split...]
    all_to_all x3 -> x0, waiting for transfers between devices: 178 us -> none  [the longest x1 77.1 us: shards(): lax.all_to_all(result, 'expert', split_axis=0, concat_axis=0, tiled=True)]
    all_to_all x1, waiting for transfers between devices: 0.01 us -> 172 us  [shards(): lax.all_to_all(result.reshape(received.shape), 'expert', split_axis=0, co...]
    all_to_all x3 -> x0, starting transfers between devices: 48.3 us -> none  [the longest x1 29.8 us: shards(): lax.all_to_all(result, 'expert', split_axis=0, concat_axis=0, tiled=True)]
    slice x3 -> x2, local copies, waits for them, and re-layouts: 12.6 us -> 0.01 us  [the longest x1 0.01 us: shards(): out_one = combine(attn_one, back, spot_one, kept_one, gates[0])]
    another operation x5 -> x1, local copies, waits for them, and re-layouts: 13 us -> 0.68 us  [the longest x3 10.3 us: shards(): jnp.stack([first_out.reshape(first_rows.shape), second_out.reshape(second...]
    reshape x5 -> x2, local copies, waits for them, and re-layouts: 26.9 us -> 17.1 us  [the longest x1 8.71 us: shards(): back = lax.all_to_all(result.reshape(received.shape), 'expert', split_axi...]
  transfers between devices with their start and end apart: 7 -> 1, of which waited for: 6 -> 1; matrix products, arithmetic and copies ran while one was open for 17% -> 0% of each run, Pallas kernels for 0% -> 0%
where the time goes in v1:
time: 488 us; the launch traced here: 484 us
  blocking collectives  187 us (38%)
  waiting for transfers between devices  172 us (35%)
  local copies, waits for them, and re-layouts  76.9 us (16%)
  matrix products  36.7 us (8%)
  starting transfers between devices  6.68 us (1%)
    all_to_all x1, blocking collectives, shards(): lax.all_to_all(packed.reshape(width, per_dest, features), 'expert', split...  187 us
    all_to_all x1, waiting for transfers between devices, shards(): lax.all_to_all(result.reshape(received.shape), 'expert', split_axis=0, co...  172 us
    gather x4, local copies, waits for them, and re-layouts, combine(): picked = returned[jnp.minimum(spot, returned.shape[0] - 1)]  21.8 us
    dot_general x1, matrix products, expert_rows(): jnp.dot(hidden, down_mat, preferred_element_type=jnp.float32)  18.7 us
    dot_general x1, matrix products, expert_rows(): gate_val = jnp.dot(rows, gate_mat, preferred_element_type=jnp.float32)  10.4 us
  transfers between devices with their start and end apart: 1, of which 1 were waited for; matrix products, arithmetic and copies ran while one was open for 0% of the time, Pallas kernels for 0%

profile of v1, /device:TPU:8, one launch (start us, length us, event | category | flops | bytes accessed | tf_op | source)
XLA Modules:
  0.0 483.9 jit_solution(7363795534223222319)
XLA Ops:
  0.0 1.1 fusion.54
  1.6 0.9 fusion.56
  6.7 0.8 select_reduce_fusion
  8.5 2.9 scatter_custom_fusion
  11.4 2.9 scatter_fusion
  15.8 1.4 copy.49
  17.2 1.4 reshape.335
  19.1 6.5 %gather_fusion = bf16[1152,2560]{1,0:T(8,128)(2,1)} fusion(bf16[129,2560]{1,0:T(8,128)(2,1)S(1)} %concatenate.7, s32[2048]{0:T(1024)S(1)} %pad_clamp_fusion), kind=kCustom, calls=%fused_computation | custom fusion | bytes 11801088 | tf_op jit(solution)/shard_map/gather | solution.py:104
  25.6 8.4 %reshape.336 = bf16[64,18,2560]{2,1,0:T(8,128)(2,1)} reshape(bf16[1152,2560]{1,0:T(8,128)(2,1)} %gather_fusion) | data formatting | bytes 11796480 | tf_op jit(solution)/shard_map/reshape | solution.py:106
  34.0 186.6 %all_to_all.10 = bf16[64,18,2560]{2,1,0:T(8,128)(2,1)} all-to-all(bf16[64,18,2560]{2,1,0:T(8,128)(2,1)} %reshape.336), channel_id=1, replica_groups=mesh['dp'=4,'expert'=64] {'expert'}, dimensions={0} | all-to-all | bytes 11796480 | tf_op jit(solution)/shard_map/all_to_all | solution.py:105
  220.6 8.6 %reshape.337 = bf16[1152,2560]{1,0:T(8,128)(2,1)} reshape(bf16[64,18,2560]{2,1,0:T(8,128)(2,1)} %all_to_all.10) | data formatting | bytes 11796480 | tf_op jit(solution)/shard_map/reshape | solution.py:112
  229.3 10.4 %fusion.4 = f32[1152,768]{1,0:T(8,128)} fusion(bf16[1152,2560]{1,0:T(8,128)(2,1)} %reshape.337, bf16[1,2560,768]{2,1,0:T(8,128)(2,1)} %param.21), kind=kOutput, calls=%fused_computation.11 | convolution fusion | flops 4529848320 | bytes 13369344 | tf_op jit(solution)/shard_map/dot_general | solution.py:38
  239.7 18.7 %convolution_convert_fusion = bf16[1152,2560]{1,0:T(8,128)(2,1)} fusion(bf16[1,768,2560]{2,1,0:T(8,128)(2,1)} %param.23, bf16[1152,2560]{1,0:T(8,128)(2,1)} %reshape.337, bf16[1,2560,768]{2,1,0:T(8,128)(2,1)} %param.22, f32[1152,768]{1,0:T(8,128)} %fusion.4), kind=kOutput, calls=%fused_computation.7 | convolution fusion | flops 9067954176 | bytes 23199744 | tf_op jit(solution)/shard_map/dot_general | solution.py:41
  258.4 8.3 %reshape.338 = bf16[64,18,2560]{2,1,0:T(8,128)(2,1)} reshape(bf16[1152,2560]{1,0:T(8,128)(2,1)} %convolution_convert_fusion) | data formatting | bytes 11796480 | tf_op jit(solution)/shard_map/reshape | solution.py:114
  266.7 6.7 %all-to-all-start.1 = ((bf16[64,18,2560]{2,1,0:T(8,128)(2,1)}), bf16[64,18,2560]{2,1,0:T(8,128)(2,1)}, u32[]{:S(2)}, u32[]{:S(2)}) async-start(bf16[64,18,2560]{2,1,0:T(8,128)(2,1)} %reshape.338), calls=%async_computation.1 | async-start | bytes 15728640 | tf_op jit(solution)/shard_map/all_to_all | solution.py:113
  274.1 172.3 %all-to-all-done.1 = bf16[64,18,2560]{2,1,0:T(8,128)(2,1)} async-done(((bf16[64,18,2560]{2,1,0:T(8,128)(2,1)}), bf16[64,18,2560]{2,1,0:T(8,128)(2,1)}, u32[]{:S(2)}, u32[]{:S(2)}) %all-to-all-start.1) | async-done | bytes 5898272 | tf_op jit(solution)/shard_map/all_to_all | solution.py:113
  446.4 8.7 %reshape.339 = bf16[1152,2560]{1,0:T(8,128)(2,1)} reshape(bf16[64,18,2560]{2,1,0:T(8,128)(2,1)} %all-to-all-done.1) | data formatting | bytes 11796480 | tf_op jit(solution)/shard_map/reshape | solution.py:115
  455.1 8.6 %gather_fusion.1 = bf16[384,2560]{1,0:T(8,128)(2,1)S(1)} fusion(bf16[1152,2560]{1,0:T(8,128)(2,1)} %reshape.339, s32[1024]{0:T(1024)S(1)} %pad_clamp_fusion.2), kind=kCustom, calls=%fused_computation.1 | custom fusion | bytes 3933696 | tf_op jit(solution)/shard_map/gather | solution.py:57
  463.8 2.3 reshape.349
  466.0 2.6 fusion.69
  469.4 8.6 %gather_fusion.2 = bf16[384,2560]{1,0:T(8,128)(2,1)S(1)} fusion(bf16[1152,2560]{1,0:T(8,128)(2,1)} %reshape.339, s32[1024]{0:T(1024)S(1)} %pad_clamp_fusion.1), kind=kCustom, calls=%fused_computation.2 | custom fusion | bytes 3933696 | tf_op jit(solution)/shard_map/gather | solution.py:57
  478.0 2.3 reshape.357
  480.3 2.6 fusion.70
  483.0 0.9 pad_maximum_fusion
  (81 shorter events, 8.9 us)
Async XLA Ops:
  1.5 4.5 copy-start.3
  1.5 5.0 %copy-start.5 = (s32[4]{0:T(128)S(1)}, s32[4]{0:T(128)}, u32[]{:S(2)}) copy-start(s32[4]{0:T(128)} %param.20) | copy-start | bytes 52
  1.5 5.1 %copy-start.6 = (s32[64]{0:T(128)S(1)}, s32[64]{0:T(128)}, u32[]{:S(2)}) copy-start(s32[64]{0:T(128)} %param.19) | copy-start | bytes 772
  11.4 3.0 copy-start.1
  15.8 3.1 copy-start.2
  266.7 6.9 %copy-start.4 = (f32[2,64,6]{1,0,2:T(2,128)S(1)}, f32[2,64,6]{1,0,2:T(2,128)}, u32[]{:S(2)}) copy-start(f32[2,64,6]{1,0,2:T(2,128)} %param.17) | copy-start | bytes 9220
  266.7 179.7 %all-to-all-start.1 = ((bf16[64,18,2560]{2,1,0:T(8,128)(2,1)}), bf16[64,18,2560]{2,1,0:T(8,128)(2,1)}, u32[]{:S(2)}, u32[]{:S(2)}) async-start(bf16[64,18,2560]{2,1,0:T(8,128)(2,1)} %reshape.338), calls=%async_computation.1 | async-start | bytes 15728640 | tf_op jit(solution)/shard_map/all_to_all | solution.py:113
  480.3 2.7 copy-start
